TPU v7x, 128 devices: a whole 4x4x4 slice. The times are simulated.
128 devices in a mesh: prow: 4 (over x), pcol: 32 (over y, z, core).
Axes of the slice: x: 4, y: 4, z: 4, core: 2. Of those that a mesh axis runs over, the one named last changes fastest.
Arguments:
- matrix: float32 [128, 4, 128, 1, 32, 128], P(None, 'prow', None, None, 'pcol')
- pivots: int32 [128], replicated, may hold values from 0 to 65535, as said below
Outputs:
- factored: float32 [128, 4, 128, 1, 32, 128], P(None, 'prow', None, None, 'pcol')
Inputs may be any that keep to these rules, and one draw needn't show every extreme that they name: `pivots`: entry j lies between j and 65535; the last entry is 65535.
All inputs are finite; a program needn't handle non-finite values.
Results may differ from a plain program's by a relative error of at most 0.0001.
Values sent between devices are 32-bit elements; how exact they have to be, the bound alone decides.
A program may use at most 128 MiB of HBM per device.

v0:
```python
import jax
import jax.numpy as jnp
from jax import lax
from jax.sharding import PartitionSpec as P


def from_root(value, axis, source):
    kept = jnp.where(lax.axis_index(axis) == source, value, 0).astype(value.dtype)
    return lax.psum(kept, axis)


def eliminate(square):
    size = square.shape[0]
    positions = jnp.arange(size, dtype=jnp.int32)

    def reduce_step(column_no, factors):
        column = factors[:, column_no]
        pivot_value = factors[column_no, column_no]
        below = positions > column_no
        multiplier = jnp.where(below, column / pivot_value, 0.0)
        pivot_row = jnp.where(below, factors[column_no], 0.0)
        factors = factors - multiplier[:, None] * pivot_row[None, :]
        return jnp.where(
            below[:, None] & (positions[None, :] == column_no), multiplier[:, None], factors
        )

    return lax.fori_loop(0, size, reduce_step, square)


def both_inverses(packed):
    size = packed.shape[0]
    positions = jnp.arange(size, dtype=jnp.int32)
    strict_low = jnp.where(positions[:, None] > positions[None, :], packed, 0.0)
    strict_up = jnp.where(positions[:, None] < positions[None, :], packed, 0.0)
    diag_values = jnp.sum(jnp.where(positions[:, None] == positions[None, :], packed, 0.0), axis=1)

    def row_step(step_no, inverses):
        upper_inv, lower_inv = inverses
        low_no = jnp.asarray(step_no).astype(jnp.int32)
        up_no = (size - 1 - jnp.asarray(step_no)).astype(jnp.int32)
        low_row = lax.dynamic_index_in_dim(strict_low, low_no, 0, keepdims=False)
        up_row = lax.dynamic_index_in_dim(strict_up, up_no, 0, keepdims=False)
        pivot_value = lax.dynamic_index_in_dim(diag_values, up_no, 0, keepdims=False)
        low_unit = (positions == low_no).astype(jnp.float32)
        up_unit = (positions == up_no).astype(jnp.float32)
        new_low = low_unit - jnp.dot(
            low_row, lower_inv, precision=lax.Precision.HIGHEST, preferred_element_type=jnp.float32
        )
        new_up = (
            up_unit
            - jnp.dot(
                up_row,
                upper_inv,
                precision=lax.Precision.HIGHEST,
                preferred_element_type=jnp.float32,
            )
        ) / pivot_value
        lower_inv = lax.dynamic_update_index_in_dim(lower_inv, new_low, low_no, 0)
        upper_inv = lax.dynamic_update_index_in_dim(upper_inv, new_up, up_no, 0)
        return (upper_inv, lower_inv)

    start = jnp.zeros((size, size), jnp.float32)
    return lax.fori_loop(0, size, row_step, (start, start))


def global_index(count_items, block_size, group_count, my_place):
    positions = jnp.arange(count_items, dtype=jnp.int32)
    return (positions // block_size * group_count + my_place) * block_size + positions % block_size


def trace_sources(pivots, first_row, count, targets):

    def back_step(step_no, sources):
        column_no = (first_row + count - 1 - step_no).astype(jnp.int32)
        partner = pivots[column_no]
        return jnp.where(
            sources == column_no, partner, jnp.where(sources == partner, column_no, sources)
        )

    return lax.fori_loop(0, count, back_step, targets)


def swap_rows(held, pivots, first_row, count, block_size, prow_count, my_prow):
    rows_local = held.shape[0]
    targets = jnp.concatenate([first_row + jnp.arange(count, dtype=jnp.int32), pivots])
    sources = trace_sources(pivots, first_row, count, targets)
    source_mine = sources // block_size % prow_count == my_prow
    source_local = sources // (block_size * prow_count) * block_size + sources % block_size
    fetched = jnp.take(held, jnp.where(source_mine, source_local, 0), axis=0)
    contrib = jnp.where(source_mine[:, None], fetched, 0.0)
    moved_rows = lax.psum(contrib, "prow")
    target_mine = targets // block_size % prow_count == my_prow
    target_local = targets // (block_size * prow_count) * block_size + targets % block_size
    held = held.at[jnp.where(target_mine, target_local, rows_local)].set(moved_rows, mode="drop")
    return (held, moved_rows)


def local(matrix, pivots):
    row_blocks = matrix.shape[0]
    block_size = matrix.shape[2]
    col_blocks = matrix.shape[3]
    prow_count = lax.axis_size("prow")
    pcol_count = lax.axis_size("pcol")
    my_prow = lax.axis_index("prow")
    my_pcol = lax.axis_index("pcol")
    rows_local = row_blocks * block_size
    cols_local = col_blocks * block_size
    held = matrix.reshape(rows_local, cols_local)
    row_global = global_index(rows_local, block_size, prow_count, my_prow)
    col_global = global_index(cols_local, block_size, pcol_count, my_pcol)
    owner_prow = 0 % prow_count
    row_slot = 0 // prow_count
    owner_pcol = 0 % pcol_count
    col_slot = 0 // pcol_count
    row_lo = row_slot * block_size
    col_lo = col_slot * block_size
    held, moved_rows = swap_rows(held, pivots, 0, block_size, block_size, prow_count, my_prow)
    panel_cols = held
    diag_raw = from_root(
        held[row_lo : row_lo + block_size, col_lo : col_lo + block_size], "prow", owner_prow
    )
    row_raw = held[row_lo : row_lo + block_size]
    below = row_global >= block_size
    packed = eliminate(diag_raw)
    upper_inv, lower_inv = both_inverses(packed)
    solved_cols = jnp.dot(
        panel_cols, upper_inv, precision=lax.Precision.HIGHEST, preferred_element_type=jnp.float32
    )
    payload = jnp.concatenate([jnp.where(below[:, None], solved_cols, 0.0), packed, lower_inv], 0)
    received = from_root(payload, "pcol", owner_pcol)
    left_op = received[:rows_local]
    packed = received[rows_local : rows_local + block_size]
    lower_inv = received[rows_local + block_size :]
    solved = jnp.dot(
        lower_inv, row_raw, precision=lax.Precision.HIGHEST, preferred_element_type=jnp.float32
    )
    row_final = from_root(solved, "prow", owner_prow)
    trailing_cols = col_global >= block_size
    right_op = jnp.where(trailing_cols[None, :], row_final, 0.0)
    held = held - jnp.dot(
        left_op, right_op, precision=lax.Precision.HIGHEST, preferred_element_type=jnp.float32
    )
    panel_new = jnp.where(below[:, None], left_op, panel_cols)
    panel_tiles = panel_new.reshape(row_blocks, block_size, block_size)
    panel_tiles = panel_tiles.at[row_slot].set(
        jnp.where(my_prow == owner_prow, packed, panel_tiles[row_slot])
    )
    held = held.at[:, col_lo : col_lo + block_size].set(
        jnp.where(my_pcol == owner_pcol, panel_tiles.reshape(rows_local, block_size), held)
    )
    keep_rows = (my_prow == owner_prow) & trailing_cols[None, :]
    held = held.at[row_lo : row_lo + block_size].set(
        jnp.where(keep_rows, row_final, held[row_lo : row_lo + block_size])
    )
    return held.reshape(matrix.shape)


def solution(mesh):
    return jax.shard_map(
        local,
        mesh=mesh,
        in_specs=(P(None, "prow", None, None, "pcol", None), P()),
        out_specs=P(None, "prow", None, None, "pcol", None),
        check_vma=False,
    )
```

profile of v0, /device:TPU:0, one launch (start us, length us, event | category | flops | bytes accessed | tf_op | source)
XLA Modules:
  0.0 877.8 jit_solution(12851266730310642802)
XLA Ops:
  6.5 7.0 copy.43
  13.6 150.0 %while.53 = (s32[]{:T(128)}, s32[256]{0:T(256)S(1)}, s32[128]{0:T(128)S(1)}, s32[]{:T(128)}, s32[]{:T(128)}, /*index=5*/s32[]{:T(128)}, s32[]{:T(128)}) while((s32[]{:T(128)}, s32[256]{0:T(256)S(1)}, s32[128]{0:T(128)S(1)}, s32[]{:T(128)}, s32[]{:T(128)}, /*index=5*/s32[]{:T(128)}, s32[]{:T(128)}) %tuple.142), condition=%wide.region_1.2_spmd, body=%wide.region_0.1_spmd.sunk | while | flops 1030 | bytes 2191 | solution.py:80
  163.6 4.1 gather_fusion
  167.7 0.8 select_select_fusion
  168.6 43.9 %all-reduce.5.cloned.1.call-done = f32[256,128]{1,0:T(8,128)} async-done(((f32[256,128]{1,0:T(8,128)}), f32[256,128]{1,0:T(8,128)}) %all-reduce.5.cloned.1.call-update) | async-done | bytes 131088 | tf_op jit(solution)/shard_map/psum | solution.py:91
  212.5 8.2 scatter_fusion
  220.7 1.5 slice_select_fusion.3
  222.3 41.6 %all-reduce.7.cloned.1.call-done = f32[128,128]{1,0:T(8,128)} async-done(((f32[128,128]{1,0:T(8,128)}), f32[128,128]{1,0:T(8,128)}) %all-reduce.7.cloned.1.call-update) | async-done | bytes 65552 | tf_op jit(solution)/shard_map/psum | solution.py:9
  263.9 0.9 copy.4
  264.9 180.8 %while.54 = (s32[]{:T(128)}, f32[128,128]{0,1:T(8,128)S(1)}, s32[]{:T(128)}) while((s32[]{:T(128)}, f32[128,128]{0,1:T(8,128)S(1)}, s32[]{:T(128)}) %tuple.128), condition=%wide.region_6.7_spmd.clone.clone, body=%wide.region_5.6_spmd.clone.clone.sunk | while | flops 66434 | bytes 268349 | solution.py:27
  445.9 197.9 %while.55 = (s32[]{:T(128)}, f32[128,128]{1,0:T(8,128)S(1)}, f32[128,128]{1,0:T(8,128)S(1)}, f32[128,128]{1,0:T(8,128)S(1)}, f32[128]{0:T(128)S(1)}, /*index=5*/...) while((s32[]{:T(128)}, f32[128,128]{1,0:T(8,128)S(1)}, ...), condition=%wide.region_9.10_spmd.clone.clone, body=%wide.region_8.9_spmd.clone.clone.sunk | while | flops 394118 | bytes 136371 | solution.py:63
  446.5 0.7 fusion.73
  448.1 0.7 fusion.73
  449.6 0.7 fusion.73
  451.2 0.7 fusion.73
  452.7 0.7 fusion.73
  454.3 0.7 fusion.73
  455.8 0.7 fusion.73
  457.3 0.7 fusion.73
  458.9 0.7 fusion.73
  460.4 0.7 fusion.73
  462.0 0.7 fusion.73
  463.5 0.7 fusion.73
  465.1 0.7 fusion.73
  466.6 0.7 fusion.73
  468.2 0.7 fusion.73
  469.7 0.7 fusion.73
  471.3 0.7 fusion.73
  472.8 0.7 fusion.73
  474.3 0.7 fusion.73
  475.9 0.7 fusion.73
  477.4 0.7 fusion.73
  479.0 0.7 fusion.73
  480.5 0.7 fusion.73
  482.1 0.7 fusion.73
  483.6 0.7 fusion.73
  485.2 0.7 fusion.73
  486.7 0.7 fusion.73
  488.3 0.7 fusion.73
  489.8 0.7 fusion.73
  491.4 0.7 fusion.73
  492.9 0.7 fusion.73
  494.4 0.7 fusion.73
  496.0 0.7 fusion.73
  497.5 0.7 fusion.73
  499.1 0.7 fusion.73
  500.6 0.7 fusion.73
  502.2 0.7 fusion.73
  503.7 0.7 fusion.73
  505.3 0.7 fusion.73
  506.8 0.7 fusion.73
  508.4 0.7 fusion.73
  509.9 0.7 fusion.73
  643.8 18.9 %convolution_select_fusion = f32[16384,128]{1,0:T(8,128)S(1)} fusion(f32[16384,128]{1,0:T(8,128)} %scatter_fusion, f32[128,128]{1,0:T(8,128)S(1)} %get-tuple-element.386, pred[16384]{0:T(1024)(128)(4,1)S(1)} %fusion.29), kind=kOutput, calls=%fused_computation.32 | convolution fusion | flops 3223322624 | bytes 16859136 | tf_op jit(solution)/shard_map/dot_general | solution.py:126
  662.7 8.7 maximum_select_fusion
  671.8 120.8 %all-reduce.9.cloned.1.call-done = f32[16640,128]{1,0:T(8,128)} async-done(((f32[16640,128]{1,0:T(8,128)}), f32[16640,128]{1,0:T(8,128)}) %all-reduce.9.cloned.1.call-update) | async-done | bytes 8519696 | tf_op jit(solution)/shard_map/psum | solution.py:9
  792.6 9.8 %slice_select_fusion = f32[16384,128]{1,0:T(8,128)S(1)} fusion(f32[16384,128]{1,0:T(8,128)} %scatter_fusion, f32[16640,128]{1,0:T(8,128)} %all-reduce.9.cloned.1.call-done, pred[16384]{0:T(1024)(128)(4,1)S(1)} %fusion.29), kind=kLoop, calls=%fused_computation.35 | loop fusion | flops 2097152 | bytes 25182208 | tf_op jit(solution)/shard_map/jit(_where)/select_n | solution.py:143
  802.5 3.3 copy.39
  805.7 2.5 copy-done
  808.2 1.7 convolution_select_fusion.1
  809.9 1.5 fusion.34
  811.4 39.2 %all-reduce.11.cloned.1.call-done = f32[128,128]{1,0:T(8,128)} async-done(((f32[128,128]{1,0:T(8,128)}), f32[128,128]{1,0:T(8,128)}) %all-reduce.11.cloned.1.call-update) | async-done | bytes 65552 | tf_op jit(solution)/shard_map/psum | solution.py:9
  850.6 17.2 %fusion.17 = f32[16384,128]{1,0:T(8,128)S(1)} fusion(f32[16384,128]{1,0:T(8,128)} %bitcast.90, f32[16384,128]{1,0:T(8,128)} %scatter_fusion, f32[16640,128]{1,0:T(8,128)} %all-reduce.9.cloned.1.call-done, pred[]{:T(512)S(6)} %eq.133, f32[128,128]{1,0:T(8,128)} %all-reduce.11.cloned.1.call-done, pred[128]{0:T(512)(128)(4,1)S(1)} %fusion.49), kind=kOutput, calls=%fused_computation.31 | convolution fusion | flops 3225436160 | bytes 33620096 | tf_op jit(solution)/shard_map/dot_general | solution.py:140
  867.9 3.4 copy-done.1
  (1650 shorter events, 485.7 us)
Async XLA Ops:
  6.5 7.0 copy-start.3
  6.5 206.0 %all-reduce.5.cloned.1.call-start = ((), (), s32[]{:S(2)}) async-start(), calls=%async_computation | async-start | bytes 262144 | tf_op jit(solution)/shard_map/psum | solution.py:91
  168.5 95.4 %all-reduce.7.cloned.1.call-start = ((), (), s32[]{:S(2)}) async-start(), calls=%async_computation.1 | async-start | bytes 131072 | tf_op jit(solution)/shard_map/psum | solution.py:9
  222.2 570.4 %all-reduce.9.cloned.1.call-start = ((), (), s32[]{:S(2)}) async-start(), calls=%async_computation.2 | async-start | bytes 17039360 | tf_op jit(solution)/shard_map/psum | solution.py:9
  671.5 179.1 %all-reduce.11.cloned.1.call-start = ((), (), s32[]{:S(2)}) async-start(), calls=%async_computation.3 | async-start | bytes 131072 | tf_op jit(solution)/shard_map/psum | solution.py:9
  802.5 5.7 copy-start
  850.6 17.3 %copy-start.2 = (f32[128,128]{1,0:T(8,128)S(1)}, f32[128,128]{1,0:T(8,128)}, u32[]{:S(2)}) copy-start(f32[128,128]{1,0:T(8,128)} %all-reduce.11.cloned.1.call-done) | copy-start | bytes 196612
  867.9 3.4 copy-start.1
Sparse Core Ops, SparseCore 0:
  168.6 43.8 all-reduce.4
  222.3 41.5 all-reduce.6
  671.6 120.9 all-reduce.8
  810.0 40.5 all-reduce.10
where the time goes:
time: 881 us; the launch traced here: 878 us
  local copies, waits for them, and re-layouts  272 us (31%)
  waiting for transfers between devices  246 us (28%)
  other arithmetic  184 us (21%)
  matrix products  149 us (17%)
  loops' own time  13.9 us (2%)
  between operations  13.3 us (2%)
    psum x3, waiting for transfers between devices, from_root(): return lax.psum(kept, axis)  202 us
    dot_general x128, matrix products, row_step(): jnp.dot(up_row, upper_inv, precision=lax.Precision.HIGHEST, preferred_ele...  90.9 us
    dynamic_slice x128, local copies, waits for them, and re-layouts, reduce_step(): pivot_value = factors[column_no, column_no]  74.4 us
    dynamic_slice x128, local copies, waits for them, and re-layouts, back_step(): partner = pivots[column_no]  74.2 us
    dynamic_slice x128, local copies, waits for them, and re-layouts, row_step(): lax.dynamic_index_in_dim(diag_values, up_no, 0, keepdims=False)  74.2 us
    broadcast_in_dim x128, other arithmetic, reduce_step(): jnp.where(below[:, None] & (positions[None, :] == column_no), multiplier[...  72.6 us
    select_n x128, other arithmetic, back_step(): jnp.where(sources == column_no, partner, jnp.where(sources == partner, co...  72.6 us
    psum x1, waiting for transfers between devices, swap_rows(): moved_rows = lax.psum(contrib, 'prow')  43.9 us
  transfers between devices with their start and end apart: 4, of which 4 were waited for; matrix products, arithmetic and copies ran while one was open for 0% of the time, Pallas kernels for 0%

commit v1 on v0

--- a/solution.py
+++ b/solution.py
@@ -88,7 +88,22 @@
     source_local = sources // (block_size * prow_count) * block_size + sources % block_size
     fetched = jnp.take(held, jnp.where(source_mine, source_local, 0), axis=0)
     contrib = jnp.where(source_mine[:, None], fetched, 0.0)
-    moved_rows = lax.psum(contrib, "prow")
+
+    def close_members_all(block_here):
+        axis_total = lax.axis_size("prow")
+        arr_next, x_new = (block_here, 0)
+        while 1 << x_new < axis_total:
+            history = []
+            at = 0
+            while at < axis_total:
+                history.append((at, at ^ 1 << x_new))
+                at += 1
+            z = lax.ppermute(arr_next, "prow", perm=history)
+            arr_next = arr_next + z
+            x_new = x_new + 1
+        return arr_next
+
+    moved_rows = close_members_all(contrib)
     target_mine = targets // block_size % prow_count == my_prow
     target_local = targets // (block_size * prow_count) * block_size + targets % block_size
     held = held.at[jnp.where(target_mine, target_local, rows_local)].set(moved_rows, mode="drop")

time: 881 us -> 850 us (0.965)
  waiting for transfers between devices: 246 us -> 211 us
    psum x1 -> x0, waiting for transfers between devices: 43.9 us -> none  [swap_rows(): moved_rows = lax.psum(contrib, 'prow')]
  transfers between devices with their start and end apart: 4 -> 5, of which waited for: 4 -> 5; matrix products, arithmetic and copies ran while one was open for 0% -> 0% of each run, Pallas kernels for 0% -> 0%
where the time goes in v1:
time: 850 us; the launch traced here: 847 us
  local copies, waits for them, and re-layouts  264 us (31%)
  waiting for transfers between devices  211 us (25%)
  other arithmetic  191 us (22%)
  matrix products  149 us (18%)
  loops' own time  13.9 us (2%)
  between operations  13.3 us (2%)
    psum x3, waiting for transfers between devices, from_root(): return lax.psum(kept, axis)  204 us
    dot_general x128, matrix products, row_step(): jnp.dot(up_row, upper_inv, precision=lax.Precision.HIGHEST, preferred_ele...  90.9 us
    dynamic_slice x128, local copies, waits for them, and re-layouts, reduce_step(): pivot_value = factors[column_no, column_no]  74.4 us
    dynamic_slice x128, local copies, waits for them, and re-layouts, back_step(): partner = pivots[column_no]  74.2 us
    dynamic_slice x128, local copies, waits for them, and re-layouts, row_step(): lax.dynamic_index_in_dim(diag_values, up_no, 0, keepdims=False)  74.2 us
    broadcast_in_dim x128, other arithmetic, reduce_step(): jnp.where(below[:, None] & (positions[None, :] == column_no), multiplier[...  72.6 us
    select_n x128, other arithmetic, back_step(): jnp.where(sources == column_no, partner, jnp.where(sources == partner, co...  72.6 us
    dot_general x128, matrix products, row_step(): jnp.dot(low_row, lower_inv, precision=lax.Precision.HIGHEST, preferred_el...  20.1 us
  transfers between devices with their start and end apart: 5, of which 5 were waited for; matrix products, arithmetic and copies ran while one was open for 0% of the time, Pallas kernels for 0%

profile of v1, /device:TPU:0, one launch (start us, length us, event | category | flops | bytes accessed | tf_op | source)
XLA Modules:
  0.0 846.8 jit_solution(16616554307704564258)
XLA Ops:
  6.5 7.0 copy.42
  13.6 150.0 %while.53 = (s32[]{:T(128)}, s32[256]{0:T(256)S(1)}, s32[128]{0:T(128)S(1)}, s32[]{:T(128)}, s32[]{:T(128)}, /*index=5*/s32[]{:T(128)}, s32[]{:T(128)}) while((s32[]{:T(128)}, s32[256]{0:T(256)S(1)}, s32[128]{0:T(128)S(1)}, s32[]{:T(128)}, s32[]{:T(128)}, /*index=5*/s32[]{:T(128)}, s32[]{:T(128)}) %tuple.140), condition=%wide.region_1.2_spmd, body=%wide.region_0.1_spmd.sunk | while | flops 1030 | bytes 2191 | solution.py:80
  163.6 4.1 gather_fusion
  167.8 1.7 collective-permute-start
  169.5 3.5 collective-permute-done
  173.1 3.4 collective-permute-start.1
  176.5 3.2 collective-permute-done.1
  179.7 7.9 scatter_custom_fusion
  187.6 1.5 slice_select_fusion.3
  189.2 43.8 %all-reduce.4.cloned.1.call-done = f32[128,128]{1,0:T(8,128)} async-done(((f32[128,128]{1,0:T(8,128)}), f32[128,128]{1,0:T(8,128)}) %all-reduce.4.cloned.1.call-update) | async-done | bytes 65552 | tf_op jit(solution)/shard_map/psum | solution.py:9
  232.9 0.9 copy.4
  233.9 180.8 %while.54 = (s32[]{:T(128)}, f32[128,128]{0,1:T(8,128)S(1)}, s32[]{:T(128)}) while((s32[]{:T(128)}, f32[128,128]{0,1:T(8,128)S(1)}, s32[]{:T(128)}) %tuple.128), condition=%wide.region_5.6_spmd.clone.clone, body=%wide.region_4.5_spmd.clone.clone.sunk | while | flops 66434 | bytes 268349 | solution.py:27
  414.9 197.9 %while.55 = (s32[]{:T(128)}, f32[128,128]{1,0:T(8,128)S(1)}, f32[128,128]{1,0:T(8,128)S(1)}, f32[128,128]{1,0:T(8,128)S(1)}, f32[128]{0:T(128)S(1)}, /*index=5*/...) while((s32[]{:T(128)}, f32[128,128]{1,0:T(8,128)S(1)}, ...), condition=%wide.region_8.9_spmd.clone.clone, body=%wide.region_7.8_spmd.clone.clone.sunk | while | flops 394118 | bytes 136371 | solution.py:63
  415.5 0.7 fusion.76
  417.1 0.7 fusion.76
  418.6 0.7 fusion.76
  420.2 0.7 fusion.76
  421.7 0.7 fusion.76
  423.3 0.7 fusion.76
  424.8 0.7 fusion.76
  426.4 0.7 fusion.76
  427.9 0.7 fusion.76
  429.5 0.7 fusion.76
  431.0 0.7 fusion.76
  432.5 0.7 fusion.76
  434.1 0.7 fusion.76
  435.6 0.7 fusion.76
  437.2 0.7 fusion.76
  438.7 0.7 fusion.76
  440.3 0.7 fusion.76
  441.8 0.7 fusion.76
  443.4 0.7 fusion.76
  444.9 0.7 fusion.76
  446.5 0.7 fusion.76
  448.0 0.7 fusion.76
  449.5 0.7 fusion.76
  451.1 0.7 fusion.76
  452.6 0.7 fusion.76
  454.2 0.7 fusion.76
  455.7 0.7 fusion.76
  457.3 0.7 fusion.76
  458.8 0.7 fusion.76
  460.4 0.7 fusion.76
  461.9 0.7 fusion.76
  463.5 0.7 fusion.76
  465.0 0.7 fusion.76
  466.6 0.7 fusion.76
  468.1 0.7 fusion.76
  469.6 0.7 fusion.76
  471.2 0.7 fusion.76
  472.7 0.7 fusion.76
  474.3 0.7 fusion.76
  475.8 0.7 fusion.76
  612.8 18.9 %convolution_select_fusion = f32[16384,128]{1,0:T(8,128)S(1)} fusion(f32[16384,128]{1,0:T(8,128)} %scatter_custom_fusion, f32[128,128]{1,0:T(8,128)S(1)} %get-tuple-element.386, pred[16384]{0:T(1024)(128)(4,1)S(1)} %fusion.31), kind=kOutput, calls=%fused_computation.32 | convolution fusion | flops 3223322624 | bytes 16859136 | tf_op jit(solution)/shard_map/dot_general | solution.py:141
  631.8 8.8 %maximum_select_fusion = f32[16640,128]{1,0:T(8,128)} fusion(f32[128,128]{1,0:T(8,128)S(1)} %get-tuple-element.387, f32[128,128]{1,0:T(8,128)S(1)} %copy.5, f32[16384,128]{1,0:T(8,128)S(1)} %convolution_select_fusion, pred[]{:T(512)S(6)} %eq.133), kind=kLoop, calls=%fused_computation.33 | loop fusion | flops 6389760 | bytes 17039360 | tf_op jit(solution)/shard_map/jit(_where)/select_n | solution.py:8
  640.8 120.8 %all-reduce.6.cloned.1.call-done = f32[16640,128]{1,0:T(8,128)} async-done(((f32[16640,128]{1,0:T(8,128)}), f32[16640,128]{1,0:T(8,128)}) %all-reduce.6.cloned.1.call-update) | async-done | bytes 8519696 | tf_op jit(solution)/shard_map/psum | solution.py:9
  761.6 9.8 %slice_select_fusion = f32[16384,128]{1,0:T(8,128)S(1)} fusion(f32[16384,128]{1,0:T(8,128)} %scatter_custom_fusion, f32[16640,128]{1,0:T(8,128)} %all-reduce.6.cloned.1.call-done, pred[16384]{0:T(1024)(128)(4,1)S(1)} %fusion.31), kind=kLoop, calls=%fused_computation.35 | loop fusion | flops 2097152 | bytes 25182208 | tf_op jit(solution)/shard_map/jit(_where)/select_n | solution.py:158
  771.5 3.3 copy.38
  774.8 2.4 copy-done
  777.2 1.7 convolution_select_fusion.1
  778.9 1.5 fusion.36
  780.4 39.2 %all-reduce.8.cloned.1.call-done = f32[128,128]{1,0:T(8,128)} async-done(((f32[128,128]{1,0:T(8,128)}), f32[128,128]{1,0:T(8,128)}) %all-reduce.8.cloned.1.call-update) | async-done | bytes 65552 | tf_op jit(solution)/shard_map/psum | solution.py:9
  819.6 17.2 %fusion.17 = f32[16384,128]{1,0:T(8,128)S(1)} fusion(f32[16384,128]{1,0:T(8,128)} %bitcast.90, f32[16384,128]{1,0:T(8,128)} %scatter_custom_fusion, f32[16640,128]{1,0:T(8,128)} %all-reduce.6.cloned.1.call-done, pred[]{:T(512)S(6)} %eq.133, f32[128,128]{1,0:T(8,128)} %all-reduce.8.cloned.1.call-done, pred[128]{0:T(512)(128)(4,1)S(1)} %fusion.51), kind=kOutput, calls=%fused_computation.31 | convolution fusion | flops 3225436160 | bytes 33620096 | tf_op jit(solution)/shard_map/dot_general | solution.py:155
  836.9 3.4 copy-done.1
  (1652 shorter events, 487.3 us)
Async XLA Ops:
  6.5 7.0 copy-start.3
  6.5 226.4 %all-reduce.4.cloned.1.call-start = ((), (), s32[]{:S(2)}) async-start(), calls=%async_computation | async-start | bytes 131072 | tf_op jit(solution)/shard_map/psum | solution.py:9
  167.8 5.2 collective-permute-start
  173.1 6.6 collective-permute-start.1
  189.1 572.5 %all-reduce.6.cloned.1.call-start = ((), (), s32[]{:S(2)}) async-start(), calls=%async_computation.1 | async-start | bytes 17039360 | tf_op jit(solution)/shard_map/psum | solution.py:9
  640.5 179.1 %all-reduce.8.cloned.1.call-start = ((), (), s32[]{:S(2)}) async-start(), calls=%async_computation.2 | async-start | bytes 131072 | tf_op jit(solution)/shard_map/psum | solution.py:9
  771.5 5.7 copy-start
  819.6 17.3 %copy-start.2 = (f32[128,128]{1,0:T(8,128)S(1)}, f32[128,128]{1,0:T(8,128)}, u32[]{:S(2)}) copy-start(f32[128,128]{1,0:T(8,128)} %all-reduce.8.cloned.1.call-done) | copy-start | bytes 196612
  836.9 3.4 copy-start.1
Sparse Core Ops, SparseCore 0:
  189.2 43.7 all-reduce.3
  640.7 120.9 all-reduce.5
  779.0 40.5 all-reduce.7
